TPU v7x, 256 devices: a whole 4x4x8 slice. The times are simulated.
256 devices in a mesh: row: 16 (over z_lo, x), col: 16 (over z_hi, y, core).
Axes of the slice: x: 4, y: 4, z: 8 (z_hi: 2, z_lo: 4; z = z_hi * 4 + z_lo), core: 2. Of those that a mesh axis runs over, the one named last changes fastest.
Arguments:
- three_centre: bfloat16 [16, 16, 640, 4096], P('row', 'col'), may hold values from -0.3984375 to 0.3984375
- green_occ: bfloat16 [16, 2, 64, 64], P('row'), may hold values from -0.75 to 0.75
- green_vir: bfloat16 [16, 2, 64, 64], P('col'), may hold values from -0.75 to 0.75
- pair_live: int32 [16, 16], P('row', 'col'), may hold values 0 or 1
Outputs:
- chi_diag: float32 [16, 640, 640], P('row', 'col')
- chi_next: float32 [16, 640, 640], P('row', 'col')
All inputs are finite; a program needn't handle non-finite values. No bound on the sum of `pair_live` on one device may be relied on, other than what follows from the above.
Results may differ from a plain program's by a relative error of at most 0.013.
Values may be sent and summed in bfloat16 or wider, within the bound.
A program may use at most 128 MiB of HBM per device.

v0:
```python
import jax
import jax.numpy as jnp
from jax import lax
from jax.sharding import PartitionSpec as P


def passed_along(value, axis, by):
    size = lax.axis_size(axis)
    pairs = [(i, i + by) for i in range(size) if 0 <= i + by < size]
    return lax.ppermute(value, axis, pairs)


def contract(left, right):
    return lax.dot_general(
        left, right, (((1,), (1,)), ((), ())), preferred_element_type=jnp.float32
    )


def body(three_centre, green_occ, green_vir, pair_live):
    aux_rows = three_centre.shape[2]
    tile = green_occ.shape[2]
    live = pair_live[0, 0].astype(jnp.bfloat16)
    blocks = (three_centre[0, 0] * live).reshape(aux_rows, tile, tile)
    occ_half = jnp.einsum("pml,smn->spnl", blocks, green_occ[0], preferred_element_type=jnp.float32)
    occ_half = occ_half.astype(jnp.bfloat16).reshape(2, aux_rows, tile * tile)
    vir_half = jnp.einsum("pns,tls->tpnl", blocks, green_vir[0], preferred_element_type=jnp.float32)
    vir_half = vir_half.astype(jnp.bfloat16).reshape(2, aux_rows, tile * tile)
    from_above = passed_along(occ_half[1], "row", -1)
    stacked = jnp.concatenate([occ_half[0], from_above], axis=0)
    neighbour = passed_along(stacked, "col", 1)
    partial_value = contract(stacked, vir_half[0]) + contract(neighbour, vir_half[1])
    partial_value = partial_value.reshape(2, aux_rows, aux_rows)
    owned = lax.psum_scatter(
        partial_value.astype(jnp.bfloat16), "col", scatter_dimension=1, tiled=True
    ).astype(jnp.float32)
    return (owned[0][None], owned[1][None])


def solution(mesh):
    return jax.shard_map(
        body,
        mesh=mesh,
        in_specs=(
            P("row", "col", None, None),
            P("row", None, None, None),
            P("col", None, None, None),
            P("row", "col"),
        ),
        out_specs=(P("row", "col", None), P("row", "col", None)),
        check_vma=False,
    )
```

profile of v0, /device:TPU:7, one launch (start us, length us, event | category | flops | bytes accessed | tf_op | source)
XLA Modules:
  0.0 529.1 jit_solution(15603043808709320438)
XLA Ops:
  7.2 0.0 copy-start
  7.2 0.0 reduce-scatter.4.cloned.1.call-start
  7.2 7.8 %copy.14 = bf16[1,1,640,4096]{2,3,1,0:T(8,128)(2,1)} copy(bf16[1,1,640,4096]{3,2,1,0:T(8,128)(2,1)} %param.4) | data formatting | bytes 10485760 | tf_op args[0]
  15.7 3.0 broadcast_multiply_fusion
  18.7 0.0 copy-start.2
  18.7 2.3 copy-done.2
  21.0 0.0 copy-done
  21.0 15.1 %convert_bitcast_fusion.1 = bf16[2,640,64,64]{1,2,0,3:T(8,128)(2,1)} fusion(bf16[640,64,64,1]{0,2,1,3:T(8,128)(2,1)S(1)} %bitcast.33, bf16[1,2,64,64]{3,2,1,0:T(8,128)(2,1)S(1)} %copy-done), kind=kOutput, calls=%fused_computation.2 | convolution fusion | flops 676331520 | bytes 15745024 | tf_op jit(solution)/shard_map/pml,smn->spnl/dot_general | solution.py:24
  36.1 8.9 %fusion.5 = (bf16[1,640,64,64]{1,2,0,3:T(8,128)(2,1)}, bf16[1,640,64,64]{1,2,0,3:T(8,128)(2,1)}) fusion(bf16[2,640,64,64]{1,2,0,3:T(8,128)(2,1)} %convert_bitcast_fusion.1), kind=kLoop, calls=%fused_computation.11 | loop fusion | bytes 20971520 | tf_op jit(solution)/shard_map/slice | solution.py:29
  45.0 0.0 copy-start.4
  45.0 8.0 %copy.18 = bf16[1,640,64,64]{1,3,2,0:T(8,128)(2,1)} copy(bf16[1,640,64,64]{1,2,0,3:T(8,128)(2,1)} %get-tuple-element.5) | data formatting | bytes 10485760 | tf_op jit(solution)/shard_map/slice | solution.py:28
  53.0 2.6 collective-permute-start
  55.6 0.0 copy-done.4
  55.7 0.0 slice-start
  55.7 3.1 copy.17
  58.7 0.0 copy-start.3
  58.7 112.4 %collective-permute-done = bf16[640,4096]{0,1:T(8,128)(2,1)S(1)} collective-permute-done((bf16[640,4096]{0,1:T(8,128)(2,1)}, bf16[640,4096]{0,1:T(8,128)(2,1)S(1)}, u32[]{:S(2)}, u32[]{:S(2)}) %collective-permute-start) | collective-permute-done | bytes 5242912 | tf_op jit(solution)/shard_map/ppermute | solution.py:10
  171.1 0.0 copy-start.5
  171.1 0.0 slice-start.1
  171.1 0.0 copy-start.7
  171.1 4.5 pad_maximum_fusion
  175.7 0.0 copy-done.3
  175.7 0.9 copy-done.5
  176.6 4.6 collective-permute-start.1
  181.2 0.0 slice-done
  181.2 0.0 slice-done.1
  181.2 0.0 copy-done.7
  181.2 5.5 %convert_bitcast_fusion = bf16[2,640,64,64]{1,3,0,2:T(8,128)(2,1)} fusion(bf16[640,64,64,1]{0,2,3,1:T(8,128)(2,1)S(1)} %bitcast.36, bf16[1,2,64,64]{3,2,1,0:T(8,128)(2,1)S(1)} %copy-done.7), kind=kOutput, calls=%fused_computation.1 | convolution fusion | flops 676331520 | bytes 15745024 | tf_op jit(solution)/shard_map/pns,tls->tpnl/dot_general | solution.py:26
  186.8 0.0 slice-start.2
  186.8 9.1 %fusion.4 = (bf16[1,640,64,64]{1,3,0,2:T(8,128)(2,1)}, bf16[1,640,64,64]{1,3,0,2:T(8,128)(2,1)}) fusion(bf16[2,640,64,64]{1,3,0,2:T(8,128)(2,1)} %convert_bitcast_fusion), kind=kLoop, calls=%fused_computation.10 | loop fusion | bytes 20971520 | tf_op jit(solution)/shard_map/slice | solution.py:31
  195.9 98.5 %collective-permute-done.1 = bf16[1280,4096]{0,1:T(8,128)(2,1)} collective-permute-done((bf16[1280,4096]{0,1:T(8,128)(2,1)}, bf16[1280,4096]{0,1:T(8,128)(2,1)}, u32[]{:S(2)}, u32[]{:S(2)}) %collective-permute-start.1) | collective-permute-done | bytes 10485792 | tf_op jit(solution)/shard_map/ppermute | solution.py:10
  294.4 0.0 slice-start.3
  294.4 0.0 copy-start.6
  294.4 14.0 %fusion.7 = f32[1280,640]{1,0:T(8,128)} fusion(bf16[1280,4096]{0,1:T(8,128)(2,1)} %collective-permute-done.1, bf16[640,4096]{0,1:T(8,128)(2,1)} %bitcast.44), kind=kOutput, calls=%fused_computation.13 | convolution fusion | flops 6710886400 | bytes 19005440 | tf_op jit(solution)/shard_map/dot_general | solution.py:14
  308.4 0.0 slice-done.2
  308.4 0.0 slice-done.3
  308.4 0.0 copy-done.6
  308.4 0.0 copy-start.1
  308.4 10.3 %fusion.1 = bf16[1280,640]{1,0:T(8,128)(2,1)S(1)} fusion(f32[1280,640]{1,0:T(8,128)} %fusion.7, bf16[640,4096]{0,1:T(8,128)(2,1)S(1)} %bitcast.43, bf16[640,4096]{0,1:T(8,128)(2,1)} %copy-done.5, bf16[640,4096]{0,1:T(8,128)(2,1)S(1)} %bitcast.40), kind=kOutput, calls=%fused_computation.5 | convolution fusion | flops 6733496320 | bytes 20643840 | tf_op jit(solution)/shard_map/dot_general | solution.py:14
  318.7 1.7 copy.25
  320.4 1.5 copy.27
  321.8 0.0 reduce-scatter.4.cloned.1.call-update
  321.8 198.8 %reduce-scatter.4.cloned.1.call-done = bf16[40,1280]{1,0:T(8,128)(2,1)} async-done(((bf16[640,1280]{1,0:T(8,128)(2,1)}), bf16[40,1280]{1,0:T(8,128)(2,1)}) %reduce-scatter.4.cloned.1.call-update) | async-done | bytes 102416
  520.6 0.9 reshape.26
  521.5 0.7 fusion.6
  522.2 0.0 copy-done.1
  (3 shorter events, 0.0 us)
Async XLA Ops:
  7.2 13.8 %copy-start = (bf16[1,2,64,64]{3,2,1,0:T(8,128)(2,1)S(1)}, bf16[1,2,64,64]{3,2,1,0:T(8,128)(2,1)}, u32[]{:S(2)}) copy-start(bf16[1,2,64,64]{3,2,1,0:T(8,128)(2,1)} %param.5) | copy-start | bytes 49156
  7.2 513.4 %reduce-scatter.4.cloned.1.call-start = ((), (), s32[]{:S(2)}) async-start(), calls=%async_computation.1 | async-start | bytes 1740800
  18.7 2.3 copy-start.2
  45.0 10.6 %copy-start.4 = (bf16[1,640,64,64]{1,2,0,3:T(8,128)(2,1)S(1)}, bf16[1,640,64,64]{1,2,0,3:T(8,128)(2,1)}, u32[]{:S(2)}) copy-start(bf16[1,640,64,64]{1,2,0,3:T(8,128)(2,1)} %get-tuple-element.4) | copy-start | bytes 15728644
  53.0 118.1 %collective-permute-start = (bf16[640,4096]{0,1:T(8,128)(2,1)}, bf16[640,4096]{0,1:T(8,128)(2,1)S(1)}, u32[]{:S(2)}, u32[]{:S(2)}) collective-permute-start(bf16[640,4096]{0,1:T(8,128)(2,1)} %bitcast.7), channel_id=1, source_target_pairs={{16,0},{32,16},{48,32},{64,48},{80,64},{96,80},{112,96},{128,112},... | collective-permute-start | bytes 15728648 | tf_op jit(solution)/shard_map/ppermute | solution.py:10
  55.7 125.5 %slice-start = ((s8[5242880]{0:T(1024)(128)(4,1)}), s8[4194304]{0:T(1024)(128)(4,1)S(1)}, s32[]{:S(2)}) async-start(s8[5242880]{0:T(1024)(128)(4,1)} %bitcast.34), calls=%async_computation.2 | async-start | bytes 8388608
  58.7 116.9 %copy-start.3 = (bf16[1,640,64,64]{1,3,2,0:T(8,128)(2,1)}, bf16[1,640,64,64]{1,3,2,0:T(8,128)(2,1)S(1)}, u32[]{:S(2)}) copy-start(bf16[1,640,64,64]{1,3,2,0:T(8,128)(2,1)S(1)} %copy.17) | copy-start | bytes 15728644
  171.1 5.4 %copy-start.5 = (bf16[640,4096]{0,1:T(8,128)(2,1)}, bf16[640,4096]{0,1:T(8,128)(2,1)S(1)}, u32[]{:S(2)}) copy-start(bf16[640,4096]{0,1:T(8,128)(2,1)S(1)} %collective-permute-done) | copy-start | bytes 15728644
  171.1 10.1 %slice-start.1 = ((s8[5242880]{0:T(1024)(128)(4,1)}), s8[1048576]{0:T(1024)(128)(4,1)S(1)}, s32[]{:S(2)}) async-start(s8[5242880]{0:T(1024)(128)(4,1)} %bitcast.34), calls=%async_computation.3 | async-start | bytes 2097152
  171.1 10.1 %copy-start.7 = (bf16[1,2,64,64]{3,2,1,0:T(8,128)(2,1)S(1)}, bf16[1,2,64,64]{3,2,1,0:T(8,128)(2,1)}, u32[]{:S(2)}) copy-start(bf16[1,2,64,64]{3,2,1,0:T(8,128)(2,1)} %param.6) | copy-start | bytes 49156
  176.6 117.8 %collective-permute-start.1 = (bf16[1280,4096]{0,1:T(8,128)(2,1)}, bf16[1280,4096]{0,1:T(8,128)(2,1)}, u32[]{:S(2)}, u32[]{:S(2)}) collective-permute-start(bf16[1280,4096]{0,1:T(8,128)(2,1)} %pad_maximum_fusion), channel_id=1, source_target_pairs={{0,1},{1,2},{2,3},{3,4},{4,5},{5,6},{6,7},{7,8},{8,9},{9,10},{10,1... | collective-permute-start | bytes 31457288 | tf_op jit(solution)/shard_map/ppermute | solution.py:10
  186.8 121.6 %slice-start.2 = ((s8[5242880]{0:T(1024)(128)(4,1)}), s8[1048576]{0:T(1024)(128)(4,1)S(1)}, s32[]{:S(2)}) async-start(s8[5242880]{0:T(1024)(128)(4,1)} %bitcast.38), calls=%async_computation.4 | async-start | bytes 2097152
  294.4 14.0 %slice-start.3 = ((s8[5242880]{0:T(1024)(128)(4,1)}), s8[4194304]{0:T(1024)(128)(4,1)S(1)}, s32[]{:S(2)}) async-start(s8[5242880]{0:T(1024)(128)(4,1)} %bitcast.38), calls=%async_computation.5 | async-start | bytes 8388608
  294.4 14.0 %copy-start.6 = (bf16[1,640,64,64]{1,3,0,2:T(8,128)(2,1)S(1)}, bf16[1,640,64,64]{1,3,0,2:T(8,128)(2,1)}, u32[]{:S(2)}) copy-start(bf16[1,640,64,64]{1,3,0,2:T(8,128)(2,1)} %get-tuple-element.2) | copy-start | bytes 15728644
  308.4 213.8 %copy-start.1 = (bf16[1,2,64,64]{3,2,1,0:T(8,128)(2,1)S(1)}, bf16[1,2,64,64]{3,2,1,0:T(8,128)(2,1)}, u32[]{:S(2)}) copy-start(bf16[1,2,64,64]{3,2,1,0:T(8,128)(2,1)} %param.5) | copy-start | bytes 49156
Sparse Core Ops, SparseCore 0:
  322.0 198.5 reduce-scatter.3
where the time goes:
time: 532 us; the launch traced here: 529 us
  waiting for transfers between devices  410 us (77%)
  local copies, waits for them, and re-layouts  44.9 us (8%)
  matrix products  44.9 us (8%)
  between operations  14.8 us (3%)
  other arithmetic  7.51 us (1%)
  starting transfers between devices  7.29 us (1%)
    ppermute x2, waiting for transfers between devices, passed_along(): return lax.ppermute(value, axis, pairs)  211 us
    unnamed x2, waiting for transfers between devices  199 us
    dot_general x2, matrix products, contract(): lax.dot_general(left, right, (((1,), (1,)), ((), ())), preferred_element_...  24.3 us
    unnamed x28, local copies, waits for them, and re-layouts  15.2 us
    dot_general x1, matrix products, body(): jnp.einsum('pml,smn->spnl', blocks, green_occ[0], preferred_element_type=...  15.1 us
    slice x2, local copies, waits for them, and re-layouts, body(): stacked = jnp.concatenate([occ_half[0], from_above], axis=0)  12 us
  transfers between devices with their start and end apart: 3, of which 3 were waited for; matrix products, arithmetic and copies ran while one was open for 3% of the time, Pallas kernels for 0%

commit v1 on v0

v1 whole, which is shorter than its diff:
```python
import functools

import jax
import jax.numpy as jnp
from jax import lax
from jax.experimental import pallas as pl
from jax.experimental.pallas import tpu as pltpu
from jax.sharding import PartitionSpec as P

MESH = pl.DeviceIdType.MESH
BF, F32 = jnp.bfloat16, jnp.float32
C = 128
W = 256
STEP = 1024


def dot_nt(a, b):
    return lax.dot_general(a, b, (((1,), (1,)), ((), ())), preferred_element_type=F32)


def dot_nn(a, b):
    return lax.dot_general(a, b, (((1,), (0,)), ((), ())), preferred_element_type=F32)


def kernel(
    rows, cols, tile,
    y_hbm, bdo, bdv, outd, outn,
    y, yr, yd, zt, zin, xa, xb, t32, accd, accn, bdor, bdvr, sd, sn, rd, rn,
    loc_sem, yr_s, yr_r, yd_s, yd_r, z_s, z_r, g_s, g_r, d_s, d_r, n_s, n_r,
):
    n = lax.axis_index("row")
    l = lax.axis_index("col")
    aux, width = y_hbm.shape
    nch = aux // C
    own = aux // cols
    even = lax.rem(l, 2) == 0
    odd = lax.rem(l, 2) == 1
    has_up = n < rows - 1
    has_dn = n > 0
    has_right = l < cols - 1
    has_left = l > 0
    nblk = width // W

    barrier = pltpu.get_barrier_semaphore()

    def hello(r, c):
        pl.semaphore_signal(barrier, inc=1, device_id=(r, c), device_id_type=MESH)

    def hello_col(k, _):
        hello(n, lax.rem(l + k, cols))
        return 0

    lax.fori_loop(1, cols, hello_col, 0)

    @pl.when(has_up)
    def _():
        def f(k, _):
            hello(n + 1, 2 * k)
            return 0
        lax.fori_loop(0, cols // 2, f, 0)

    @pl.when(has_dn & even)
    def _():
        def f(k, _):
            hello(n - 1, k)
            return 0
        lax.fori_loop(0, cols, f, 0)

    @pl.when(has_up & odd)
    def _():
        hello(n + 1, l)

    @pl.when(has_dn & odd)
    def _():
        hello(n - 1, l)

    up, dn, par = has_up.astype(jnp.int32), has_dn.astype(jnp.int32), lax.rem(l, 2)
    from_up = up * (cols // 2 + par)
    from_dn = dn * (cols - par * (cols - 1))
    pl.semaphore_wait(barrier, cols - 1 + from_up + from_dn)

    def chunk(ref, i):
        return ref.at[pl.ds(i * C, C), :]

    def remote(src, dst, ss, rs, r, c):
        return pltpu.make_async_remote_copy(
            src_ref=src, dst_ref=dst, send_sem=ss, recv_sem=rs, device_id=(r, c), device_id_type=MESH)

    def to_left(i):
        return remote(chunk(y_hbm, i), chunk(yr, i), yr_s.at[i], yr_r.at[i], n, l - 1)

    def to_down(i):
        return remote(chunk(y_hbm, i), chunk(yd, i), yd_s.at[i], yd_r.at[i], n - 1, l)

    def z_up(i):
        return remote(zt.at[i], zin.at[i], z_s.at[i], z_r.at[i], n + 1, l)

    gv_left = lambda: remote(bdv.at[1], bdvr, g_s.at[0], g_r.at[0], n, l - 1)
    go_down = lambda: remote(bdo.at[1], bdor, g_s.at[1], g_r.at[1], n - 1, l)

    @pl.when(has_left)
    def _():
        gv_left().start()
        for i in range(nch):
            to_left(i).start()

    @pl.when(has_dn & odd)
    def _():
        go_down().start()
        for i in range(nch):
            to_down(i).start()

    def local(i):
        return pltpu.make_async_copy(chunk(y_hbm, i), chunk(y, i), loc_sem.at[i])

    for i in range(nch):
        local(i).start()
    for i in range(nch):
        local(i).wait()

    def spread(g):
        return jnp.concatenate(
            [t32[pl.ds(g * (W // tile) + j, tile, stride=tile), :] for j in range(W // tile)], axis=0)

    def make_z(i, right):
        def one(b, _):
            at = pl.ds(b * W, W)
            z = dot_nt(bdv[0], y[pl.ds(i * C, C), at])
            if right:
                z = z + dot_nt(bdvr[...], yr[pl.ds(i * C, C), at])
            t32[at, :] = z
            return 0
        lax.fori_loop(0, nblk, one, 0)

        def two(g, _):
            zt[i, pl.ds(g * W, W), :] = spread(g).astype(BF)
            return 0
        lax.fori_loop(0, nblk, two, 0)

    def make_x(src, i, targets):
        def one(b, _):
            at = pl.ds(b * W, W)
            t32[at, :] = dot_nt(bdo[2], src[pl.ds(i * C, C), at])
            return 0
        lax.fori_loop(0, nblk, one, 0)

        def two(g, _):
            part = jnp.transpose(spread(g)).astype(BF)
            for green, dst in targets:
                dst[pl.ds(i * C, C), pl.ds(g * W, W)] = dot_nn(part, green()).astype(BF)
            return 0
        lax.fori_loop(0, nblk, two, 0)

    def chi_cols(acc, i, x, z):
        acc[i] = jnp.zeros((aux, C), F32)

        def one(k, _):
            at = pl.ds(k * STEP, STEP)
            acc[i] += dot_nn(x[:, at], z[i, at, :])
            return 0
        lax.fori_loop(0, width // STEP, one, 0)

    def chi_tile(acc, p, q, x, z):
        at_p = pl.ds(p * C, C)
        acc[q, at_p, :] = dot_nn(x[at_p, :], z[q])

    def piece(send, recv, ss, rs, i, r, c):
        return remote(send.at[i, c], recv.at[i, l], ss.at[i, c], rs.at[i, l], r, c)

    def fill(acc, send, i):
        for d in range(cols):
            send[i, d] = acc[i, d * own:(d + 1) * own, :].astype(BF)

    def scatter_d(i):
        fill(accd, sd, i)
        rd[i, l] = sd[i, l]

        def one(k, _):
            piece(sd, rd, d_s, d_r, i, n, lax.rem(l + k, cols)).start()
            return 0
        lax.fori_loop(1, cols, one, 0)

    def scatter_n_even(i):
        fill(accn, sn, i)

        def one(k, _):
            piece(sn, rn, n_s, n_r, i, n - 1, k).start()
            return 0
        lax.fori_loop(0, cols, one, 0)

    def scatter_n_odd(i):
        fill(accn, sn, i)
        rn[i, l] = sn[i, l]

        def one(k, _):
            piece(sn, rn, n_s, n_r, i, n, lax.rem(l + k, cols)).start()
            return 0
        lax.fori_loop(1, cols, one, 0)

    def each(f):
        def g(i, _):
            f(i)
            return 0
        lax.fori_loop(0, nch, g, 0)

    @pl.when(even)
    def _():
        remote(bdv.at[1], bdvr, g_s.at[0], g_r.at[0], n, l).wait_recv()

        def first(i):
            remote(chunk(y_hbm, i), chunk(yr, i), yr_s.at[i], yr_r.at[i], n, l).wait_recv()
            make_z(i, True)

            @pl.when(has_up)
            def _():
                z_up(i).start()
        each(first)
        each(lambda i: make_x(y, i, ((lambda: bdo[0], xa), (lambda: bdo[1], xb))))

        def second(i):
            chi_cols(accd, i, xa, zt)
            scatter_d(i)
        each(second)

        @pl.when(has_dn)
        def _():
            def third(i):
                remote(zt.at[i], zin.at[i], z_s.at[i], z_r.at[i], n, l).wait_recv()
                chi_cols(accn, i, xb, zin)
                scatter_n_even(i)
            each(third)

    @pl.when(odd)
    def _():
        each(lambda i: make_x(y, i, ((lambda: bdo[0], xa),)))

        @pl.when(has_right)
        def _():
            remote(bdv.at[1], bdvr, g_s.at[0], g_r.at[0], n, l).wait_recv()

        @pl.when(has_up)
        def _():
            remote(bdo.at[1], bdor, g_s.at[1], g_r.at[1], n, l).wait_recv()

        def step(i):
            @pl.when(has_right)
            def _():
                remote(chunk(y_hbm, i), chunk(yr, i), yr_s.at[i], yr_r.at[i], n, l).wait_recv()
                make_z(i, True)

            @pl.when(jnp.logical_not(has_right))
            def _():
                make_z(i, False)
            chi_cols(accd, i, xa, zt)
            scatter_d(i)

            @pl.when(has_up)
            def _():
                remote(chunk(y_hbm, i), chunk(yd, i), yd_s.at[i], yd_r.at[i], n, l).wait_recv()
                make_x(yd, i, ((lambda: bdor[...], xb),))

                def a(p, _):
                    chi_tile(accn, p, i, xb, zt)
                    return 0
                lax.fori_loop(0, i + 1, a, 0)

                def b(q, _):
                    chi_tile(accn, i, q, xb, zt)
                    return 0
                lax.fori_loop(0, i, b, 0)
        each(step)

        @pl.when(has_up)
        def _():
            each(scatter_n_odd)

    def add_up(recv, out):
        for i in range(nch):
            total = recv[i, 0].astype(F32)
            for j in range(1, cols):
                total = total + recv[i, j].astype(F32)
            out[:, i * C:(i + 1) * C] = total

    def got_d(i):
        def one(k, _):
            j = lax.rem(l + k, cols)
            remote(sd.at[i, j], rd.at[i, j], d_s.at[i, j], d_r.at[i, j], n, l).wait_recv()
            return 0
        lax.fori_loop(1, cols, one, 0)
    each(got_d)
    add_up(rd, outd)

    @pl.when(has_up)
    def _():
        def got_n(i):
            def one(k, _):
                remote(sn.at[i, k], rn.at[i, k], n_s.at[i, k], n_r.at[i, k], n, l).wait_recv()
                return 0

            @pl.when(even)
            def _():
                lax.fori_loop(0, cols, one, 0)

            @pl.when(odd)
            def _():
                lax.fori_loop(1, cols, lambda k, c: one(lax.rem(l + k, cols), c), 0)
        each(got_n)
        add_up(rn, outn)

    @pl.when(jnp.logical_not(has_up))
    def _():
        outn[...] = jnp.zeros_like(outn)

    @pl.when(has_left)
    def _():
        gv_left().wait_send()
        for i in range(nch):
            to_left(i).wait_send()

    @pl.when(has_dn & odd)
    def _():
        go_down().wait_send()
        for i in range(nch):
            to_down(i).wait_send()

    @pl.when(has_up & even)
    def _():
        for i in range(nch):
            z_up(i).wait_send()

    def sent(send, recv, ss, rs, i, first, r):
        def one(k, _):
            piece(send, recv, ss, rs, i, r, lax.rem(l + k, cols)).wait_send()
            return 0
        lax.fori_loop(first, cols, one, 0)

    each(lambda i: sent(sd, rd, d_s, d_r, i, 1, n))

    @pl.when(has_dn & even)
    def _():
        each(lambda i: sent(sn, rn, n_s, n_r, i, 0, n - 1))

    @pl.when(has_up & odd)
    def _():
        each(lambda i: sent(sn, rn, n_s, n_r, i, 1, n))


def solution(mesh):
    rows, cols = mesh.shape["row"], mesh.shape["col"]

    def body(three_centre, green_occ, green_vir, pair_live):
        aux, width = three_centre.shape[2:]
        tile = green_occ.shape[2]
        nch, own = aux // C, aux // cols
        live = pair_live[0, 0].astype(BF)
        eye = jnp.eye(W // tile, dtype=BF)

        def diagonal(g):
            wide = eye[None, :, None, :, None] * g[:, None, :, None, :]
            return wide.reshape(g.shape[0], W, W)

        bdo = jnp.concatenate([diagonal(green_occ[0] * live), jnp.eye(W, dtype=BF)[None]], axis=0)
        bdv = diagonal(green_vir[0] * live)
        dma = pltpu.SemaphoreType.DMA
        vm = lambda *s: pltpu.VMEM(s, BF)
        outd, outn = pl.pallas_call(
            functools.partial(kernel, rows, cols, tile),
            out_shape=[jax.ShapeDtypeStruct((own, aux), F32)] * 2,
            in_specs=[
                pl.BlockSpec(memory_space=pl.ANY),
                pl.BlockSpec(memory_space=pltpu.VMEM),
                pl.BlockSpec(memory_space=pltpu.VMEM),
            ],
            out_specs=[pl.BlockSpec(memory_space=pltpu.VMEM)] * 2,
            scratch_shapes=[
                vm(aux, width), vm(aux, width), vm(aux, width),
                vm(nch, width, C), vm(nch, width, C),
                vm(aux, width), vm(aux, width),
                pltpu.VMEM((width, C), F32),
                pltpu.VMEM((nch, aux, C), F32), pltpu.VMEM((nch, aux, C), F32),
                vm(W, W), vm(W, W),
                vm(nch, cols, own, C), vm(nch, cols, own, C),
                vm(nch, cols, own, C), vm(nch, cols, own, C),
                dma((nch,)), dma((nch,)), dma((nch,)), dma((nch,)), dma((nch,)), dma((nch,)), dma((nch,)),
                dma((2,)), dma((2,)),
                dma((nch, cols)), dma((nch, cols)), dma((nch, cols)), dma((nch, cols)),
            ],
            compiler_params=pltpu.CompilerParams(
                collective_id=0, has_side_effects=True, vmem_limit_bytes=60 * 1024 * 1024),
        )(three_centre[0, 0], bdo, bdv)
        return outd[None], outn[None]

    return jax.shard_map(
        body,
        mesh=mesh,
        in_specs=(
            P("row", "col", None, None),
            P("row", None, None, None),
            P("col", None, None, None),
            P("row", "col"),
        ),
        out_specs=(P("row", "col", None), P("row", "col", None)),
        check_vma=False,
    )
```

time: 532 us -> 240 us (0.45)
  the two profiles are of different devices: /device:TPU:7 before, /device:TPU:161 now
where the time goes in v1:
time: 240 us; the launch traced here: 239 us
  Pallas kernels  231 us (96%)
  local copies, waits for them, and re-layouts  4.38 us (2%)
    pallas_call x1, Pallas kernels, body(): pl.pallas_call(functools.partial(kernel, rows, cols, tile), out_shape=[ja...  231 us

profile of v1, /device:TPU:161, one launch (start us, length us, event | category | flops | bytes accessed | tf_op | source)
XLA Modules:
  0.0 239.4 jit_solution(2511439357302085334)
XLA Ops:
  1.3 0.8 multiply_bitcast_fusion
  2.1 0.1 mul.70
  2.2 0.3 mul.71
  2.5 0.1 mul.75
  2.7 0.3 mul.76
  3.0 0.1 mul.64
  3.2 0.2 mul.65
  3.4 0.7 broadcast_multiply_fusion
  4.2 0.8 pad_maximum_fusion.bdo
  5.0 231.4 %shard_map.59 = (f32[40,640]{1,0:T(8,128)}, f32[40,640]{1,0:T(8,128)}) custom-call(bf16[640,4096]{1,0:T(8,128)(2,1)} %bitcast.8, bf16[3,256,256]{2,1,0:T(8,128)(2,1)} %pad_maximum_fusion.bdo, bf16[2,256,256]{2,1,0:T(8,128)(2,1)} %get-tuple-element.6.bdv), custom_call_target="tpu_custom_call" | custom-call | tf_op jit(solution)/shard_map/pallas_call | solution.py:366
  236.3 1.5 copy.9
  237.9 1.5 copy.10
  (2 shorter events, 0.0 us)

commit v2 on v1

v2 whole, which is shorter than its diff:
```python
import functools

import jax
import jax.numpy as jnp
from jax import lax
from jax.experimental import pallas as pl
from jax.experimental.pallas import tpu as pltpu
from jax.sharding import PartitionSpec as P

MESH = pl.DeviceIdType.MESH
BF, F32 = jnp.bfloat16, jnp.float32
C = 128
W = 256
STEP = 1024


def dot_nt(a, b):
    return lax.dot_general(a, b, (((1,), (1,)), ((), ())), preferred_element_type=F32)


def dot_nn(a, b):
    return lax.dot_general(a, b, (((1,), (0,)), ((), ())), preferred_element_type=F32)


def kernel(
    rows, cols, tile,
    y_hbm, bdo, bdv, outd, outn,
    y, yr, yd, zt, zin, xa, xb, t32, accd, accn, bdor, bdvr, rel,
    s0d, s0n, r0d, r0n, sad, san, rad, ran, sbd, sbn, rbd, rbn,
    loc_sem, yr_s, yr_r, yd_s, yd_r, z_s, z_r, g_s, g_r, rel_s, rel_r, part_s, part_r,
    d0_s, d0_r, n0_s, n0_r, da_s, da_r, na_s, na_r, db_s, db_r, nb_s, nb_r,
):
    n = lax.axis_index("row")
    l = lax.axis_index("col")
    aux, width = y_hbm.shape
    nch = aux // C
    own = aux // cols
    half = cols // 2
    ny = half // 2
    core = lax.rem(l, 2)
    iy = lax.rem(l // 2, ny)
    iz = l // half
    even = core == 0
    odd = core == 1
    has_up = n < rows - 1
    has_dn = n > 0
    has_right = l < cols - 1
    has_left = l > 0
    nblk = width // W
    wpart = width // ny
    is_src = l == half
    is_dst = l == half - 1
    is_rel = (l > half) & even

    barrier = pltpu.get_barrier_semaphore()

    def hello(cond, r, c):
        @pl.when(cond)
        def _():
            pl.semaphore_signal(barrier, inc=1, device_id=(r, c), device_id_type=MESH)
        return cond.astype(jnp.int32)

    def y_peer(k):
        return iz * half + lax.rem(iy + k, ny) * 2 + core

    z_peer = lax.rem(l + half, cols)
    always = l >= 0
    count = hello(has_left, n, l - 1) + hello(has_right, n, l + 1)
    count += hello(has_up, n + 1, l) + hello(has_dn, n - 1, l)
    count += hello(has_dn & even, n - 1, l + 1) + hello(has_up & odd, n + 1, l - 1)
    count += hello(always, n, z_peer) + hello(is_rel, n, half - 1)
    for k in range(1, ny):
        count += hello(always, n, y_peer(k)) + hello(is_dst, n, half + 2 * k)
    pl.semaphore_wait(barrier, count)

    def chunk(ref, i):
        return ref.at[pl.ds(i * C, C), :]

    def remote(src, dst, ss, rs, r, c):
        return pltpu.make_async_remote_copy(
            src_ref=src, dst_ref=dst, send_sem=ss, recv_sem=rs, device_id=(r, c), device_id_type=MESH)

    def to_left(i):
        return remote(chunk(y_hbm, i), chunk(yr, i), yr_s.at[i], yr_r.at[i], n, l - 1)

    def to_down(i):
        return remote(chunk(y_hbm, i), chunk(yd, i), yd_s.at[i], yd_r.at[i], n - 1, l)

    def z_up(i):
        return remote(zt.at[i], zin.at[i], z_s.at[i], z_r.at[i], n + 1, l)

    gv_left = lambda: remote(bdv.at[1], bdvr, g_s.at[0], g_r.at[0], n, l - 1)
    go_down = lambda: remote(bdo.at[1], bdor, g_s.at[1], g_r.at[1], n - 1, l)

    def cut(ref, i, k):
        return ref.at[pl.ds(i * C, C), pl.ds(k * wpart, wpart)]

    def part_direct(i):
        return remote(cut(y_hbm, i, 0), cut(yr, i, 0), part_s.at[i, 0], part_r.at[i, 0], n, l - 1)

    def part_out(i, k):
        return remote(cut(y_hbm, i, k), rel.at[i], part_s.at[i, k], rel_r.at[i], n, half + 2 * k)

    def part_on(i, k):
        return remote(rel.at[i], cut(yr, i, k), rel_s.at[i], part_r.at[i, k], n, half - 1)

    @pl.when(has_left)
    def _():
        gv_left().start()

    @pl.when(is_src)
    def _():
        for i in range(nch):
            part_direct(i).start()
            for k in range(1, ny):
                part_out(i, k).start()

    @pl.when(has_left & jnp.logical_not(is_src))
    def _():
        for i in range(nch):
            to_left(i).start()

    @pl.when(has_dn & odd)
    def _():
        go_down().start()
        for i in range(nch):
            to_down(i).start()

    def local(i):
        return pltpu.make_async_copy(chunk(y_hbm, i), chunk(y, i), loc_sem.at[i])

    for i in range(nch):
        local(i).start()
    for i in range(nch):
        local(i).wait()

    def spread(g):
        return jnp.concatenate(
            [t32[pl.ds(g * (W // tile) + j, tile, stride=tile), :] for j in range(W // tile)], axis=0)

    def make_z(i, right):
        def one(b, _):
            at = pl.ds(b * W, W)
            z = dot_nt(bdv[0], y[pl.ds(i * C, C), at])
            if right:
                z = z + dot_nt(bdvr[...], yr[pl.ds(i * C, C), at])
            t32[at, :] = z
            return 0
        lax.fori_loop(0, nblk, one, 0, unroll=True)

        def two(g, _):
            zt[i, pl.ds(g * W, W), :] = spread(g).astype(BF)
            return 0
        lax.fori_loop(0, nblk, two, 0, unroll=True)

    def make_x(src, i, targets):
        def one(b, _):
            at = pl.ds(b * W, W)
            t32[at, :] = jnp.transpose(src[pl.ds(i * C, C), at].astype(F32))
            return 0
        lax.fori_loop(0, nblk, one, 0, unroll=True)

        def two(g, _):
            part = jnp.transpose(spread(g)).astype(BF)
            for green, dst in targets:
                dst[pl.ds(i * C, C), pl.ds(g * W, W)] = dot_nn(part, green()).astype(BF)
            return 0
        lax.fori_loop(0, nblk, two, 0, unroll=True)

    def chi_cols(acc, i, x, z):
        acc[i] = jnp.zeros((aux, C), F32)

        def one(k, _):
            at = pl.ds(k * STEP, STEP)
            acc[i] += dot_nn(x[:, at], z[i, at, :])
            return 0
        lax.fori_loop(0, width // STEP, one, 0)

    def chi_tile(acc, p, q, x, z):
        at_p = pl.ds(p * C, C)
        acc[q, at_p, :] = dot_nn(x[at_p, :], z[q])

    def fill(acc, s0, i):
        for d in range(cols):
            s0[i, d % 2, d // 2] = acc[i, d * own:(d + 1) * own, :].astype(BF)

    def d0(i):
        return remote(s0d.at[i, 1 - core], r0d.at[i], d0_s.at[i], d0_r.at[i], n, l + 1 - 2 * core)

    def n0_even(i, c):
        return remote(s0n.at[i, c], r0n.at[i, 0], n0_s.at[i, c], n0_r.at[i, 0], n - 1, l + c)

    def n0_odd(i):
        return remote(s0n.at[i, 0], r0n.at[i, 1], n0_s.at[i, 0], n0_r.at[i, 1], n, l - 1)

    def scatter_d(i):
        fill(accd, s0d, i)
        d0(i).start()

    def scatter_n_even(i):
        fill(accn, s0n, i)
        n0_even(i, 0).start()
        n0_even(i, 1).start()

    def scatter_n_odd(i):
        fill(accn, s0n, i)
        n0_odd(i).start()

    def a_copy(sa, ra, ss, rs, i, k):
        to = lax.rem(iy + k, ny)
        return remote(sa.at[i, to], ra.at[i, iy], ss.at[i, to], rs.at[i, iy], n, y_peer(k))

    def a_send(first, second, sa, ra, ss, rs, i):
        for z in range(2):
            for k in range(ny):
                at = z * ny + k
                sa[i, k, z] = (first(at).astype(F32) + second(at).astype(F32)).astype(BF)
        ra[i, iy] = sa[i, iy]
        for k in range(1, ny):
            a_copy(sa, ra, ss, rs, i, k).start()

    def a_d(i):
        d0(i).wait_recv()
        a_send(lambda at: s0d[i, core, at], lambda at: r0d[i, at], sad, rad, da_s, da_r, i)

    def a_n(i):
        n0_even(i, 0).wait_recv()

        @pl.when(even)
        def _():
            n0_odd(i).wait_recv()
            a_send(lambda at: r0n[i, 0, at], lambda at: r0n[i, 1, at], san, ran, na_s, na_r, i)

        @pl.when(odd)
        def _():
            a_send(lambda at: r0n[i, 0, at], lambda at: s0n[i, 1, at], san, ran, na_s, na_r, i)

    def b_copy(sb, rb, ss, rs, i):
        return remote(sb.at[i], rb.at[i], ss.at[i], rs.at[i], n, z_peer)

    def b_send(sa, ra, sas, sar, sb, rb, ss, rs, out, i):
        for k in range(1, ny):
            j = lax.rem(iy + k, ny)
            remote(sa.at[i, j], ra.at[i, j], sas.at[i, j], sar.at[i, j], n, l).wait_recv()

        def total(z):
            t = ra[i, 0, z].astype(F32)
            for j in range(1, ny):
                t = t + ra[i, j, z].astype(F32)
            return t
        sb[i] = total(1 - iz).astype(BF)
        b_copy(sb, rb, ss, rs, i).start()
        out[:, pl.ds(pl.multiple_of(i * C, C), C)] = total(iz)

    def b_d(i):
        b_send(sad, rad, da_s, da_r, sbd, rbd, db_s, db_r, outd, i)

    def b_n(i):
        b_send(san, ran, na_s, na_r, sbn, rbn, nb_s, nb_r, outn, i)

    def last(sb, rb, ss, rs, out, i):
        b_copy(sb, rb, ss, rs, i).wait_recv()
        out[:, pl.ds(pl.multiple_of(i * C, C), C)] += rb[i].astype(F32)

    def settle(i):
        @pl.when(i >= 1)
        def _():
            a_d(i - 1)

        @pl.when(i >= 2)
        def _():
            b_d(i - 2)

    def each(f):
        def g(i, _):
            f(i)
            return 0
        lax.fori_loop(0, nch, g, 0)

    def right_chunk(i):
        return remote(chunk(y_hbm, i), chunk(yr, i), yr_s.at[i], yr_r.at[i], n, l)

    @pl.when(even)
    def _():
        remote(bdv.at[1], bdvr, g_s.at[0], g_r.at[0], n, l).wait_recv()

        def first(i):
            right_chunk(i).wait_recv()
            make_z(i, True)

            @pl.when(has_up)
            def _():
                z_up(i).start()

            @pl.when(is_rel)
            def _():
                part_out(i, 1).wait_recv()
                part_on(i, iy).start()
        each(first)
        each(lambda i: make_x(y, i, ((lambda: bdo[0], xa), (lambda: bdo[1], xb))))

        def second(i):
            chi_cols(accd, i, xa, zt)
            scatter_d(i)
        each(second)

        def third(i):
            @pl.when(has_dn)
            def _():
                remote(zt.at[i], zin.at[i], z_s.at[i], z_r.at[i], n, l).wait_recv()
                chi_cols(accn, i, xb, zin)
                scatter_n_even(i)
            settle(i)
        each(third)

    @pl.when(odd)
    def _():
        each(lambda i: make_x(y, i, ((lambda: bdo[0], xa),)))

        @pl.when(has_right)
        def _():
            remote(bdv.at[1], bdvr, g_s.at[0], g_r.at[0], n, l).wait_recv()

        @pl.when(has_up)
        def _():
            remote(bdo.at[1], bdor, g_s.at[1], g_r.at[1], n, l).wait_recv()

        def step(i):
            @pl.when(has_right)
            def _():
                @pl.when(is_dst)
                def _():
                    for k in range(ny):
                        remote(cut(y_hbm, i, k), cut(yr, i, k), part_s.at[i, k], part_r.at[i, k], n, l).wait_recv()

                @pl.when(jnp.logical_not(is_dst))
                def _():
                    right_chunk(i).wait_recv()
                make_z(i, True)

            @pl.when(jnp.logical_not(has_right))
            def _():
                make_z(i, False)
            chi_cols(accd, i, xa, zt)
            scatter_d(i)

            @pl.when(has_up)
            def _():
                remote(chunk(y_hbm, i), chunk(yd, i), yd_s.at[i], yd_r.at[i], n, l).wait_recv()
                make_x(yd, i, ((lambda: bdor[...], xb),))

                def a(p, _):
                    chi_tile(accn, p, i, xb, zt)
                    return 0
                lax.fori_loop(0, i + 1, a, 0)

                def b(q, _):
                    chi_tile(accn, i, q, xb, zt)
                    return 0
                lax.fori_loop(0, i, b, 0)
            settle(i)
        each(step)

        @pl.when(has_up)
        def _():
            each(scatter_n_odd)

    a_d(nch - 1)

    @pl.when(has_up)
    def _():
        each(a_n)
    b_d(nch - 2)
    b_d(nch - 1)

    @pl.when(has_up)
    def _():
        each(b_n)
    each(lambda i: last(sbd, rbd, db_s, db_r, outd, i))

    @pl.when(has_up)
    def _():
        each(lambda i: last(sbn, rbn, nb_s, nb_r, outn, i))

    @pl.when(jnp.logical_not(has_up))
    def _():
        outn[...] = jnp.zeros_like(outn)

    @pl.when(has_left)
    def _():
        gv_left().wait_send()

    @pl.when(is_src)
    def _():
        for i in range(nch):
            part_direct(i).wait_send()
            for k in range(1, ny):
                part_out(i, k).wait_send()

    @pl.when(is_rel)
    def _():
        for i in range(nch):
            part_on(i, iy).wait_send()

    @pl.when(has_left & jnp.logical_not(is_src))
    def _():
        for i in range(nch):
            to_left(i).wait_send()

    @pl.when(has_dn & odd)
    def _():
        go_down().wait_send()
        for i in range(nch):
            to_down(i).wait_send()

    @pl.when(has_up & even)
    def _():
        for i in range(nch):
            z_up(i).wait_send()

    def sent_d(i):
        d0(i).wait_send()
        b_copy(sbd, rbd, db_s, db_r, i).wait_send()
        for k in range(1, ny):
            a_copy(sad, rad, da_s, da_r, i, k).wait_send()
    each(sent_d)

    @pl.when(has_up)
    def _():
        def sent_n(i):
            b_copy(sbn, rbn, nb_s, nb_r, i).wait_send()
            for k in range(1, ny):
                a_copy(san, ran, na_s, na_r, i, k).wait_send()
        each(sent_n)

    @pl.when(has_dn & even)
    def _():
        each(lambda i: (n0_even(i, 0).wait_send(), n0_even(i, 1).wait_send()))

    @pl.when(has_up & odd)
    def _():
        each(lambda i: n0_odd(i).wait_send())


def solution(mesh):
    rows, cols = mesh.shape["row"], mesh.shape["col"]

    def body(three_centre, green_occ, green_vir, pair_live):
        aux, width = three_centre.shape[2:]
        tile = green_occ.shape[2]
        nch, own = aux // C, aux // cols
        half = cols // 2
        ny = half // 2
        live = pair_live[0, 0].astype(BF)
        eye = jnp.eye(W // tile, dtype=BF)

        def diagonal(g):
            wide = eye[None, :, None, :, None] * g[:, None, :, None, :]
            return wide.reshape(g.shape[0], W, W)

        bdo = diagonal(green_occ[0] * live)
        bdv = diagonal(green_vir[0] * live)
        dma = pltpu.SemaphoreType.DMA
        vm = lambda *s: pltpu.VMEM(s, BF)
        outd, outn = pl.pallas_call(
            functools.partial(kernel, rows, cols, tile),
            out_shape=[jax.ShapeDtypeStruct((own, aux), F32)] * 2,
            in_specs=[
                pl.BlockSpec(memory_space=pl.ANY),
                pl.BlockSpec(memory_space=pltpu.VMEM),
                pl.BlockSpec(memory_space=pltpu.VMEM),
            ],
            out_specs=[pl.BlockSpec(memory_space=pltpu.VMEM)] * 2,
            scratch_shapes=[
                vm(aux, width), vm(aux, width), vm(aux, width),
                vm(nch, width, C), vm(nch, width, C),
                vm(aux, width), vm(aux, width),
                pltpu.VMEM((width, C), F32),
                pltpu.VMEM((nch, aux, C), F32), pltpu.VMEM((nch, aux, C), F32),
                vm(W, W), vm(W, W), vm(nch, C, width // ny),
                vm(nch, 2, half, own, C), vm(nch, 2, half, own, C), vm(nch, half, own, C), vm(nch, 2, half, own, C),
                vm(nch, ny, 2, own, C), vm(nch, ny, 2, own, C), vm(nch, ny, 2, own, C), vm(nch, ny, 2, own, C),
                vm(nch, own, C), vm(nch, own, C), vm(nch, own, C), vm(nch, own, C),
                *[dma((nch,))] * 7,
                dma((2,)), dma((2,)), dma((nch,)), dma((nch,)), dma((nch, ny)), dma((nch, ny)),
                dma((nch,)), dma((nch,)), dma((nch, 2)), dma((nch, 2)),
                *[dma((nch, ny))] * 4, *[dma((nch,))] * 4,
            ],
            compiler_params=pltpu.CompilerParams(
                collective_id=0, has_side_effects=True, vmem_limit_bytes=60 * 1024 * 1024),
        )(three_centre[0, 0], bdo, bdv)
        return outd[None], outn[None]

    return jax.shard_map(
        body,
        mesh=mesh,
        in_specs=(
            P("row", "col", None, None),
            P("row", None, None, None),
            P("col", None, None, None),
            P("row", "col"),
        ),
        out_specs=(P("row", "col", None), P("row", "col", None)),
        check_vma=False,
    )
```

time: 240 us -> 137 us (0.57)
  the two profiles are of different devices: /device:TPU:161 before, /device:TPU:7 now
where the time goes in v2:
time: 137 us; the launch traced here: 135 us
  Pallas kernels  128 us (93%)
  local copies, waits for them, and re-layouts  4.38 us (3%)
  other arithmetic  1.62 us (1%)
    pallas_call x1, Pallas kernels, body(): pl.pallas_call(functools.partial(kernel, rows, cols, tile), out_shape=[ja...  128 us
    unnamed x2, local copies, waits for them, and re-layouts  3.09 us

profile of v2, /device:TPU:7, one launch (start us, length us, event | category | flops | bytes accessed | tf_op | source)
XLA Modules:
  0.0 135.0 jit_solution(631437385093696428)
XLA Ops:
  1.3 0.8 multiply_bitcast_fusion
  2.1 0.1 mul.70
  2.2 0.3 mul.71
  2.5 0.1 mul.75
  2.7 0.3 mul.76
  3.0 0.1 mul.64
  3.2 0.2 mul.65
  3.4 0.8 broadcast_multiply_fusion
  4.2 127.7 %shard_map.59 = (f32[40,640]{1,0:T(8,128)}, f32[40,640]{1,0:T(8,128)}) custom-call(bf16[640,4096]{1,0:T(8,128)(2,1)} %bitcast.8, bf16[2,256,256]{2,1,0:T(8,128)(2,1)} %get-tuple-element.7.bdo, bf16[2,256,256]{2,1,0:T(8,128)(2,1)} %get-tuple-element.6.bdv), custom_call_target="tpu_custom_call" | custom-call | tf_op jit(solution)/shard_map/pallas_call | solution.py:465
  131.9 1.5 %copy.9 = f32[1,40,640]{2,1,0:T(8,128)} copy(f32[1,40,640]{2,1,0:T(8,128)} %bitcast.10) | data formatting | bytes 204800
  133.5 1.5 %copy.10 = f32[1,40,640]{2,1,0:T(8,128)} copy(f32[1,40,640]{2,1,0:T(8,128)} %bitcast.9) | data formatting | bytes 204800
  (1 shorter events, 0.0 us)

commit v3 on v2

--- a/solution.py
+++ b/solution.py
@@ -1,4 +1,5 @@
 import functools
+import math
 
 import jax
 import jax.numpy as jnp
@@ -22,12 +23,19 @@
     return lax.dot_general(a, b, (((1,), (0,)), ((), ())), preferred_element_type=F32)
 
 
+def shares(width, ny):
+    through = [k for k in range(ny) if k != 1 or ny < 3]
+    edges = [width // 128 * j // len(through) * 128 for j in range(len(through) + 1)]
+    return {k: (edges[j], edges[j + 1] - edges[j]) for j, k in enumerate(through)}
+
+
 def kernel(
-    rows, cols, tile,
+    rows, cols, nx, tile,
     y_hbm, bdo, bdv, outd, outn,
-    y, yr, yd, zt, zin, xa, xb, t32, accd, accn, bdor, bdvr, rel,
+    y, yr, yd, zt, zin, xa, xb, t32, accd, accn, bdor, bdvr, rel, rely, relz,
     s0d, s0n, r0d, r0n, sad, san, rad, ran, sbd, sbn, rbd, rbn,
     loc_sem, yr_s, yr_r, yd_s, yd_r, z_s, z_r, g_s, g_r, rel_s, rel_r, part_s, part_r,
+    ry_s, ry_r, yw_s, yw_r, rz_s, rz_r, zw_s, zw_r,
     d0_s, d0_r, n0_s, n0_r, da_s, da_r, na_s, na_r, db_s, db_r, nb_s, nb_r,
 ):
     n = lax.axis_index("row")
@@ -47,10 +55,17 @@
     has_right = l < cols - 1
     has_left = l > 0
     nblk = width // W
-    wpart = width // ny
+    parts = shares(width, ny)
     is_src = l == half
     is_dst = l == half - 1
-    is_rel = (l > half) & even
+    through = [k for k in parts if k > 0]
+    is_rel = l < 0
+    for k in through:
+        is_rel = is_rel | (l == half + 2 * k)
+
+    lead, tail = lax.rem(n, nx) == 0, lax.rem(n, nx) == nx - 1
+    src_y, rel_y, dst_y = odd & lead & has_dn, odd & tail & (n >= nx), odd & tail & has_up
+    src_z, rel_z, dst_z = even & tail & has_up, even & lead & (n + nx < rows), even & lead & has_dn
 
     barrier = pltpu.get_barrier_semaphore()
 
@@ -69,8 +84,14 @@
     count += hello(has_up, n + 1, l) + hello(has_dn, n - 1, l)
     count += hello(has_dn & even, n - 1, l + 1) + hello(has_up & odd, n + 1, l - 1)
     count += hello(always, n, z_peer) + hello(is_rel, n, half - 1)
+    count += hello(src_y, n + nx - 1, l) + hello(rel_y, n - nx + 1, l)
+    count += hello(rel_y, n - nx, l) + hello(dst_y, n + nx, l)
+    count += hello(src_z, n - nx + 1, l) + hello(rel_z, n + nx - 1, l)
+    count += hello(rel_z, n + nx, l) + hello(dst_z, n - nx, l)
     for k in range(1, ny):
-        count += hello(always, n, y_peer(k)) + hello(is_dst, n, half + 2 * k)
+        count += hello(always, n, y_peer(k))
+    for k in through:
+        count += hello(is_dst, n, half + 2 * k)
     pl.semaphore_wait(barrier, count)
 
     def chunk(ref, i):
@@ -93,16 +114,17 @@
     go_down = lambda: remote(bdo.at[1], bdor, g_s.at[1], g_r.at[1], n - 1, l)
 
     def cut(ref, i, k):
-        return ref.at[pl.ds(i * C, C), pl.ds(k * wpart, wpart)]
+        at, size = parts[k]
+        return ref.at[pl.ds(i * C, C), pl.ds(at, size)]
 
     def part_direct(i):
         return remote(cut(y_hbm, i, 0), cut(yr, i, 0), part_s.at[i, 0], part_r.at[i, 0], n, l - 1)
 
     def part_out(i, k):
-        return remote(cut(y_hbm, i, k), rel.at[i], part_s.at[i, k], rel_r.at[i], n, half + 2 * k)
+        return remote(cut(y_hbm, i, k), rel.at[i, :, pl.ds(0, parts[k][1])], part_s.at[i, k], rel_r.at[i], n, half + 2 * k)
 
     def part_on(i, k):
-        return remote(rel.at[i], cut(yr, i, k), rel_s.at[i], part_r.at[i, k], n, half - 1)
+        return remote(rel.at[i, :, pl.ds(0, parts[k][1])], cut(yr, i, k), rel_s.at[i], part_r.at[i, k], n, half - 1)
 
     @pl.when(has_left)
     def _():
@@ -112,7 +134,7 @@
     def _():
         for i in range(nch):
             part_direct(i).start()
-            for k in range(1, ny):
+            for k in through:
                 part_out(i, k).start()
 
     @pl.when(has_left & jnp.logical_not(is_src))
@@ -120,9 +142,45 @@
         for i in range(nch):
             to_left(i).start()
 
+    def side_y(ref, i, h):
+        return ref.at[pl.ds(i * C, C), pl.ds(h * (width // 2), width // 2)]
+
+    def side_z(ref, i, h):
+        return ref.at[i, pl.ds(h * (width // 2), width // 2), :]
+
+    def yw_direct(i):
+        return remote(side_y(y_hbm, i, 0), side_y(yd, i, 0), yw_s.at[i, 0], yw_r.at[i, 0], n - 1, l)
+
+    def yw_out(i):
+        return remote(side_y(y_hbm, i, 1), rely.at[i], yw_s.at[i, 1], ry_r.at[i], n + nx - 1, l)
+
+    def yw_on(i):
+        return remote(rely.at[i], side_y(yd, i, 1), ry_s.at[i], yw_r.at[i, 1], n - nx, l)
+
+    def zw_direct(i):
+        return remote(side_z(zt, i, 0), side_z(zin, i, 0), zw_s.at[i, 0], zw_r.at[i, 0], n + 1, l)
+
+    def zw_out(i):
+        return remote(side_z(zt, i, 1), relz.at[i], zw_s.at[i, 1], rz_r.at[i], n - nx + 1, l)
+
+    def zw_on(i):
+        return remote(relz.at[i], side_z(zin, i, 1), rz_s.at[i], zw_r.at[i, 1], n + nx, l)
+
+    plain_y = has_dn & odd & jnp.logical_not(lead)
+    plain_z = has_up & even & jnp.logical_not(tail)
+
     @pl.when(has_dn & odd)
     def _():
         go_down().start()
+
+    @pl.when(src_y)
+    def _():
+        for i in range(nch):
+            yw_direct(i).start()
+            yw_out(i).start()
+
+    @pl.when(plain_y)
+    def _():
         for i in range(nch):
             to_down(i).start()
 
@@ -267,10 +325,6 @@
         def _():
             a_d(i - 1)
 
-        @pl.when(i >= 2)
-        def _():
-            b_d(i - 2)
-
     def each(f):
         def g(i, _):
             f(i)
@@ -288,16 +342,29 @@
             right_chunk(i).wait_recv()
             make_z(i, True)
 
-            @pl.when(has_up)
+            @pl.when(plain_z)
             def _():
                 z_up(i).start()
 
-            @pl.when(is_rel)
-            def _():
-                part_out(i, 1).wait_recv()
-                part_on(i, iy).start()
+            @pl.when(src_z)
+            def _():
+                zw_direct(i).start()
+                zw_out(i).start()
+
+            for k in through:
+                @pl.when(l == half + 2 * k)
+                def _():
+                    part_out(i, k).wait_recv()
+                    part_on(i, k).start()
         each(first)
         each(lambda i: make_x(y, i, ((lambda: bdo[0], xa), (lambda: bdo[1], xb))))
+
+        def pass_z(i):
+            @pl.when(rel_z)
+            def _():
+                zw_out(i).wait_recv()
+                zw_on(i).start()
+        pass_z(0)
 
         def second(i):
             chi_cols(accd, i, xa, zt)
@@ -307,10 +374,21 @@
         def third(i):
             @pl.when(has_dn)
             def _():
-                remote(zt.at[i], zin.at[i], z_s.at[i], z_r.at[i], n, l).wait_recv()
+                @pl.when(lead)
+                def _():
+                    zw_direct(i).wait_recv()
+                    zw_on(i).wait_recv()
+
+                @pl.when(jnp.logical_not(lead))
+                def _():
+                    remote(zt.at[i], zin.at[i], z_s.at[i], z_r.at[i], n, l).wait_recv()
                 chi_cols(accn, i, xb, zin)
                 scatter_n_even(i)
             settle(i)
+
+            @pl.when(i < nch - 1)
+            def _():
+                pass_z(i + 1)
         each(third)
 
     @pl.when(odd)
@@ -326,11 +404,16 @@
             remote(bdo.at[1], bdor, g_s.at[1], g_r.at[1], n, l).wait_recv()
 
         def step(i):
+            @pl.when(rel_y)
+            def _():
+                yw_out(i).wait_recv()
+                yw_on(i).start()
+
             @pl.when(has_right)
             def _():
                 @pl.when(is_dst)
                 def _():
-                    for k in range(ny):
+                    for k in parts:
                         remote(cut(y_hbm, i, k), cut(yr, i, k), part_s.at[i, k], part_r.at[i, k], n, l).wait_recv()
 
                 @pl.when(jnp.logical_not(is_dst))
@@ -346,7 +429,14 @@
 
             @pl.when(has_up)
             def _():
-                remote(chunk(y_hbm, i), chunk(yd, i), yd_s.at[i], yd_r.at[i], n, l).wait_recv()
+                @pl.when(tail)
+                def _():
+                    yw_direct(i).wait_recv()
+                    yw_on(i).wait_recv()
+
+                @pl.when(jnp.logical_not(tail))
+                def _():
+                    remote(chunk(y_hbm, i), chunk(yd, i), yd_s.at[i], yd_r.at[i], n, l).wait_recv()
                 make_x(yd, i, ((lambda: bdor[...], xb),))
 
                 def a(p, _):
@@ -370,8 +460,7 @@
     @pl.when(has_up)
     def _():
         each(a_n)
-    b_d(nch - 2)
-    b_d(nch - 1)
+    each(b_d)
 
     @pl.when(has_up)
     def _():
@@ -394,13 +483,14 @@
     def _():
         for i in range(nch):
             part_direct(i).wait_send()
-            for k in range(1, ny):
+            for k in through:
                 part_out(i, k).wait_send()
 
-    @pl.when(is_rel)
-    def _():
-        for i in range(nch):
-            part_on(i, iy).wait_send()
+    for k in through:
+        @pl.when(l == half + 2 * k)
+        def _():
+            for i in range(nch):
+                part_on(i, k).wait_send()
 
     @pl.when(has_left & jnp.logical_not(is_src))
     def _():
@@ -410,13 +500,38 @@
     @pl.when(has_dn & odd)
     def _():
         go_down().wait_send()
+
+    @pl.when(plain_y)
+    def _():
         for i in range(nch):
             to_down(i).wait_send()
 
-    @pl.when(has_up & even)
+    @pl.when(plain_z)
     def _():
         for i in range(nch):
             z_up(i).wait_send()
+
+    @pl.when(src_y)
+    def _():
+        for i in range(nch):
+            yw_direct(i).wait_send()
+            yw_out(i).wait_send()
+
+    @pl.when(src_z)
+    def _():
+        for i in range(nch):
+            zw_direct(i).wait_send()
+            zw_out(i).wait_send()
+
+    @pl.when(rel_y)
+    def _():
+        for i in range(nch):
+            yw_on(i).wait_send()
+
+    @pl.when(rel_z)
+    def _():
+        for i in range(nch):
+            zw_on(i).wait_send()
 
     def sent_d(i):
         d0(i).wait_send()
@@ -451,6 +566,7 @@
         nch, own = aux // C, aux // cols
         half = cols // 2
         ny = half // 2
+        nx = math.isqrt(rows)
         live = pair_live[0, 0].astype(BF)
         eye = jnp.eye(W // tile, dtype=BF)
 
@@ -463,7 +579,7 @@
         dma = pltpu.SemaphoreType.DMA
         vm = lambda *s: pltpu.VMEM(s, BF)
         outd, outn = pl.pallas_call(
-            functools.partial(kernel, rows, cols, tile),
+            functools.partial(kernel, rows, cols, nx, tile),
             out_shape=[jax.ShapeDtypeStruct((own, aux), F32)] * 2,
             in_specs=[
                 pl.BlockSpec(memory_space=pl.ANY),
@@ -477,12 +593,13 @@
                 vm(aux, width), vm(aux, width),
                 pltpu.VMEM((width, C), F32),
                 pltpu.VMEM((nch, aux, C), F32), pltpu.VMEM((nch, aux, C), F32),
-                vm(W, W), vm(W, W), vm(nch, C, width // ny),
+                vm(W, W), vm(W, W), vm(nch, C, max(size for _, size in shares(width, ny).values())), vm(nch, C, width // 2), vm(nch, width // 2, C),
                 vm(nch, 2, half, own, C), vm(nch, 2, half, own, C), vm(nch, half, own, C), vm(nch, 2, half, own, C),
                 vm(nch, ny, 2, own, C), vm(nch, ny, 2, own, C), vm(nch, ny, 2, own, C), vm(nch, ny, 2, own, C),
                 vm(nch, own, C), vm(nch, own, C), vm(nch, own, C), vm(nch, own, C),
                 *[dma((nch,))] * 7,
                 dma((2,)), dma((2,)), dma((nch,)), dma((nch,)), dma((nch, ny)), dma((nch, ny)),
+                dma((nch,)), dma((nch,)), dma((nch, 2)), dma((nch, 2)), dma((nch,)), dma((nch,)), dma((nch, 2)), dma((nch, 2)),
                 dma((nch,)), dma((nch,)), dma((nch, 2)), dma((nch, 2)),
                 *[dma((nch, ny))] * 4, *[dma((nch,))] * 4,
             ],

time: 137 us -> 121 us (0.88)
  Pallas kernels: 128 us -> 112 us
    pallas_call x1, Pallas kernels: 128 us -> 112 us  [body(): pl.pallas_call(functools.partial(kernel, rows, cols, nx, tile), out_shape...]
where the time goes in v3:
time: 121 us; the launch traced here: 120 us
  Pallas kernels  112 us (93%)
  local copies, waits for them, and re-layouts  4.38 us (4%)
  other arithmetic  1.62 us (1%)
  between operations  1.33 us (1%)
    pallas_call x1, Pallas kernels, body(): pl.pallas_call(functools.partial(kernel, rows, cols, nx, tile), out_shape...  112 us
    unnamed x2, local copies, waits for them, and re-layouts  3.09 us

profile of v3, /device:TPU:7, one launch (start us, length us, event | category | flops | bytes accessed | tf_op | source)
XLA Modules:
  0.0 119.6 jit_solution(8949160212143537391)
XLA Ops:
  1.3 0.8 multiply_bitcast_fusion
  2.1 0.1 mul.70
  2.2 0.3 mul.71
  2.5 0.1 mul.75
  2.7 0.3 mul.76
  3.0 0.1 mul.64
  3.2 0.2 mul.65
  3.4 0.8 broadcast_multiply_fusion
  4.2 112.3 %shard_map.59 = (f32[40,640]{1,0:T(8,128)}, f32[40,640]{1,0:T(8,128)}) custom-call(bf16[640,4096]{1,0:T(8,128)(2,1)} %bitcast.8, bf16[2,256,256]{2,1,0:T(8,128)(2,1)} %get-tuple-element.7.bdo, bf16[2,256,256]{2,1,0:T(8,128)(2,1)} %get-tuple-element.6.bdv), custom_call_target="tpu_custom_call" | custom-call | tf_op jit(solution)/shard_map/pallas_call | solution.py:581
  116.6 1.5 %copy.9 = f32[1,40,640]{2,1,0:T(8,128)} copy(f32[1,40,640]{2,1,0:T(8,128)} %bitcast.10) | data formatting | bytes 204800
  118.1 1.5 %copy.10 = f32[1,40,640]{2,1,0:T(8,128)} copy(f32[1,40,640]{2,1,0:T(8,128)} %bitcast.9) | data formatting | bytes 204800
  (1 shorter events, 0.0 us)

commit v4 on v3

--- a/solution.py
+++ b/solution.py
@@ -24,15 +24,15 @@
 
 
 def shares(width, ny):
-    through = [k for k in range(ny) if k != 1 or ny < 3]
-    edges = [width // 128 * j // len(through) * 128 for j in range(len(through) + 1)]
-    return {k: (edges[j], edges[j + 1] - edges[j]) for j, k in enumerate(through)}
+    weight = [1 if k == 1 and ny > 2 else 3 for k in range(ny)]
+    edges = [width // 128 * sum(weight[:k]) // sum(weight) * 128 for k in range(ny + 1)]
+    return {k: (edges[k], edges[k + 1] - edges[k]) for k in range(ny)}
 
 
 def kernel(
     rows, cols, nx, tile,
-    y_hbm, bdo, bdv, outd, outn,
-    y, yr, yd, zt, zin, xa, xb, t32, accd, accn, bdor, bdvr, rel, rely, relz,
+    y_hbm, green_o, green_v, live, out2,
+    bdo, bdv, y, yr, yd, zt, zin, xa, xb, t32, accd, accn, bdor, bdvr, rel, rely, relz,
     s0d, s0n, r0d, r0n, sad, san, rad, ran, sbd, sbn, rbd, rbn,
     loc_sem, yr_s, yr_r, yd_s, yd_r, z_s, z_r, g_s, g_r, rel_s, rel_r, part_s, part_r,
     ry_s, ry_r, yw_s, yw_r, rz_s, rz_r, zw_s, zw_r,
@@ -41,6 +41,7 @@
     n = lax.axis_index("row")
     l = lax.axis_index("col")
     aux, width = y_hbm.shape
+    outd, outn = out2.at[0], out2.at[1]
     nch = aux // C
     own = aux // cols
     half = cols // 2
@@ -92,6 +93,14 @@
         count += hello(always, n, y_peer(k))
     for k in through:
         count += hello(is_dst, n, half + 2 * k)
+    on = live[0, 0].astype(F32)
+    spot = [lax.shift_right_logical(lax.broadcasted_iota(jnp.int32, (W, W), k), tile.bit_length() - 1) for k in range(2)]
+    for green, wide in ((green_o, bdo), (green_v, bdv)):
+        for k in range(2):
+            g = green[k].astype(F32) * on
+            g = jnp.concatenate([g] * (W // tile), axis=1)
+            g = jnp.concatenate([g] * (W // tile), axis=0)
+            wide[k] = jnp.where(spot[0] == spot[1], g, 0.0).astype(BF)
     pl.semaphore_wait(barrier, count)
 
     def chunk(ref, i):
@@ -357,18 +366,30 @@
                     part_out(i, k).wait_recv()
                     part_on(i, k).start()
         each(first)
-        each(lambda i: make_x(y, i, ((lambda: bdo[0], xa), (lambda: bdo[1], xb))))
 
         def pass_z(i):
             @pl.when(rel_z)
             def _():
                 zw_out(i).wait_recv()
                 zw_on(i).start()
-        pass_z(0)
+
+        def halves(i):
+            make_x(y, i, ((lambda: bdo[0], xa), (lambda: bdo[1], xb)))
+            for at, k in ((2, 0), (4, 1)):
+                @pl.when(i == min(at, nch - 1))
+                def _():
+                    if k < nch:
+                        pass_z(k)
+        each(halves)
 
         def second(i):
             chi_cols(accd, i, xa, zt)
             scatter_d(i)
+            for at, k in ((1, 2), (4, 3)):
+                @pl.when(i == min(at, nch - 1))
+                def _():
+                    if k < nch:
+                        pass_z(k)
         each(second)
 
         def third(i):
@@ -386,9 +407,10 @@
                 scatter_n_even(i)
             settle(i)
 
-            @pl.when(i < nch - 1)
-            def _():
-                pass_z(i + 1)
+            if nch > 4:
+                @pl.when(i == 1)
+                def _():
+                    pass_z(4)
         each(third)
 
     @pl.when(odd)
@@ -403,12 +425,14 @@
         def _():
             remote(bdo.at[1], bdor, g_s.at[1], g_r.at[1], n, l).wait_recv()
 
-        def step(i):
+        def pass_y(i):
             @pl.when(rel_y)
             def _():
                 yw_out(i).wait_recv()
                 yw_on(i).start()
-
+        pass_y(0)
+
+        def step(i):
             @pl.when(has_right)
             def _():
                 @pl.when(is_dst)
@@ -426,6 +450,10 @@
                 make_z(i, False)
             chi_cols(accd, i, xa, zt)
             scatter_d(i)
+
+            @pl.when(i < nch - 1)
+            def _():
+                pass_y(i + 1)
 
             @pl.when(has_up)
             def _():
@@ -567,27 +595,20 @@
         half = cols // 2
         ny = half // 2
         nx = math.isqrt(rows)
-        live = pair_live[0, 0].astype(BF)
-        eye = jnp.eye(W // tile, dtype=BF)
-
-        def diagonal(g):
-            wide = eye[None, :, None, :, None] * g[:, None, :, None, :]
-            return wide.reshape(g.shape[0], W, W)
-
-        bdo = diagonal(green_occ[0] * live)
-        bdv = diagonal(green_vir[0] * live)
         dma = pltpu.SemaphoreType.DMA
         vm = lambda *s: pltpu.VMEM(s, BF)
-        outd, outn = pl.pallas_call(
+        out = pl.pallas_call(
             functools.partial(kernel, rows, cols, nx, tile),
-            out_shape=[jax.ShapeDtypeStruct((own, aux), F32)] * 2,
+            out_shape=jax.ShapeDtypeStruct((2, own, aux), F32),
             in_specs=[
                 pl.BlockSpec(memory_space=pl.ANY),
                 pl.BlockSpec(memory_space=pltpu.VMEM),
                 pl.BlockSpec(memory_space=pltpu.VMEM),
+                pl.BlockSpec(memory_space=pltpu.SMEM),
             ],
-            out_specs=[pl.BlockSpec(memory_space=pltpu.VMEM)] * 2,
+            out_specs=pl.BlockSpec(memory_space=pltpu.VMEM),
             scratch_shapes=[
+                vm(2, W, W), vm(2, W, W),
                 vm(aux, width), vm(aux, width), vm(aux, width),
                 vm(nch, width, C), vm(nch, width, C),
                 vm(aux, width), vm(aux, width),
@@ -605,8 +626,8 @@
             ],
             compiler_params=pltpu.CompilerParams(
                 collective_id=0, has_side_effects=True, vmem_limit_bytes=60 * 1024 * 1024),
-        )(three_centre[0, 0], bdo, bdv)
-        return outd[None], outn[None]
+        )(three_centre[0, 0], green_occ[0], green_vir[0], pair_live)
+        return out[0][None], out[1][None]
 
     return jax.shard_map(
         body,

time: 121 us -> 115 us (0.950)
  local copies, waits for them, and re-layouts: 4.38 us -> 1.64 us
  other arithmetic: 1.62 us -> 0 us
    unnamed x2 -> x0, local copies, waits for them, and re-layouts: 3.09 us -> none
    slice x0 -> x1, local copies, waits for them, and re-layouts: none -> 1.64 us  [body(): return (out[0][None], out[1][None])]
    mul x2 -> x0, other arithmetic: 1.62 us -> none  [the longest x1 0.83 us: diagonal(): wide = eye[None, :, None, :, None] * g[:, None, :, None, :]]
    pallas_call x1, Pallas kernels: 112 us -> 111 us  [body(): pl.pallas_call(functools.partial(kernel, rows, cols, nx, tile), out_shape...]
    mul x6 -> x0, local copies, waits for them, and re-layouts: 1.29 us -> none  [diagonal(): wide = eye[None, :, None, :, None] * g[:, None, :, None, :]]
where the time goes in v4:
time: 115 us; the launch traced here: 114 us
  Pallas kernels  111 us (97%)
  local copies, waits for them, and re-layouts  1.64 us (1%)
  between operations  1.29 us (1%)
    pallas_call x1, Pallas kernels, body(): pl.pallas_call(functools.partial(kernel, rows, cols, nx, tile), out_shape...  111 us

profile of v4, /device:TPU:7, one launch (start us, length us, event | category | flops | bytes accessed | tf_op | source)
XLA Modules:
  0.0 113.7 jit_solution(3936854251735284680)
XLA Ops:
  1.3 110.7 %shard_map.59 = f32[2,40,640]{2,1,0:T(8,128)} custom-call(bf16[640,4096]{1,0:T(8,128)(2,1)} %bitcast.3, bf16[2,64,64]{2,1,0:T(8,128)(2,1)} %bitcast.4, bf16[2,64,64]{2,1,0:T(8,128)(2,1)} %bitcast.5, s32[1,1]{1,0:T(1,128)S(6)} %copy.6.live), custom_call_target="tpu_custom_call" | custom-call | tf_op jit(solution)/shard_map/pallas_call | solution.py:600
  112.0 1.6 %fusion = (f32[1,40,640]{2,1,0:T(8,128)}, f32[1,40,640]{2,1,0:T(8,128)}) fusion(f32[2,40,640]{2,1,0:T(8,128)} %shard_map.59), kind=kLoop, calls=%fused_computation | loop fusion | bytes 409600 | tf_op jit(solution)/shard_map/slice | solution.py:630

commit v5 on v4

--- a/solution.py
+++ b/solution.py
@@ -24,7 +24,7 @@
 
 
 def shares(width, ny):
-    weight = [1 if k == 1 and ny > 2 else 3 for k in range(ny)]
+    weight = [2 if k == 1 and ny > 2 else 3 for k in range(ny)]
     edges = [width // 128 * sum(weight[:k]) // sum(weight) * 128 for k in range(ny + 1)]
     return {k: (edges[k], edges[k + 1] - edges[k]) for k in range(ny)}
 
@@ -185,8 +185,11 @@
     @pl.when(src_y)
     def _():
         for i in range(nch):
-            yw_direct(i).start()
-            yw_out(i).start()
+            if i == nch - 1:
+                to_down(i).start()
+            else:
+                yw_direct(i).start()
+                yw_out(i).start()
 
     @pl.when(plain_y)
     def _():
@@ -334,6 +337,10 @@
         def _():
             a_d(i - 1)
 
+        @pl.when(i == nch - 1)
+        def _():
+            lax.fori_loop(0, nch - 2, lambda k, c: (b_d(k), c)[1], 0)
+
     def each(f):
         def g(i, _):
             f(i)
@@ -378,7 +385,7 @@
             for at, k in ((2, 0), (4, 1)):
                 @pl.when(i == min(at, nch - 1))
                 def _():
-                    if k < nch:
+                    if k < nch - 1:
                         pass_z(k)
         each(halves)
 
@@ -388,11 +395,13 @@
             for at, k in ((1, 2), (4, 3)):
                 @pl.when(i == min(at, nch - 1))
                 def _():
-                    if k < nch:
+                    if k < nch - 1:
                         pass_z(k)
         each(second)
 
         def third(i):
+            settle(i)
+
             @pl.when(has_dn)
             def _():
                 @pl.when(lead)
@@ -405,12 +414,12 @@
                     remote(zt.at[i], zin.at[i], z_s.at[i], z_r.at[i], n, l).wait_recv()
                 chi_cols(accn, i, xb, zin)
                 scatter_n_even(i)
-            settle(i)
 
             if nch > 4:
-                @pl.when(i == 1)
+                @pl.when(i == 2)
                 def _():
                     pass_z(4)
+
         each(third)
 
     @pl.when(odd)
@@ -451,44 +460,48 @@
             chi_cols(accd, i, xa, zt)
             scatter_d(i)
 
-            @pl.when(i < nch - 1)
-            def _():
-                pass_y(i + 1)
-
             @pl.when(has_up)
             def _():
-                @pl.when(tail)
-                def _():
-                    yw_direct(i).wait_recv()
-                    yw_on(i).wait_recv()
-
-                @pl.when(jnp.logical_not(tail))
-                def _():
-                    remote(chunk(y_hbm, i), chunk(yd, i), yd_s.at[i], yd_r.at[i], n, l).wait_recv()
-                make_x(yd, i, ((lambda: bdor[...], xb),))
-
                 def a(p, _):
                     chi_tile(accn, p, i, xb, zt)
                     return 0
-                lax.fori_loop(0, i + 1, a, 0)
+                lax.fori_loop(0, i, a, 0)
+
+            settle(i)
+
+            @pl.when(i < nch - 2)
+            def _():
+                pass_y(i + 1)
+
+            @pl.when(has_up)
+            def _():
+                @pl.when(tail & (i < nch - 1))
+                def _():
+                    yw_direct(i).wait_recv()
+                    yw_on(i).wait_recv()
+
+                @pl.when(jnp.logical_not(tail & (i < nch - 1)))
+                def _():
+                    remote(chunk(y_hbm, i), chunk(yd, i), yd_s.at[i], yd_r.at[i], n, l).wait_recv()
+                make_x(yd, i, ((lambda: bdor[...], xb),))
 
                 def b(q, _):
                     chi_tile(accn, i, q, xb, zt)
+
+                    @pl.when(i == nch - 1)
+                    def _():
+                        scatter_n_odd(q)
                     return 0
-                lax.fori_loop(0, i, b, 0)
-            settle(i)
+                lax.fori_loop(0, i + 1, b, 0)
         each(step)
 
-        @pl.when(has_up)
-        def _():
-            each(scatter_n_odd)
-
     a_d(nch - 1)
 
     @pl.when(has_up)
     def _():
         each(a_n)
-    each(b_d)
+    b_d(nch - 2)
+    b_d(nch - 1)
 
     @pl.when(has_up)
     def _():
@@ -541,9 +554,10 @@
 
     @pl.when(src_y)
     def _():
-        for i in range(nch):
+        for i in range(nch - 1):
             yw_direct(i).wait_send()
             yw_out(i).wait_send()
+        to_down(nch - 1).wait_send()
 
     @pl.when(src_z)
     def _():
@@ -553,7 +567,7 @@
 
     @pl.when(rel_y)
     def _():
-        for i in range(nch):
+        for i in range(nch - 1):
             yw_on(i).wait_send()
 
     @pl.when(rel_z)

time: 115 us -> 111 us (0.965); the launches traced: 114 us -> 111 us
  Pallas kernels: 111 us -> 108 us
    pallas_call x1, Pallas kernels: 111 us -> 108 us  [body(): pl.pallas_call(functools.partial(kernel, rows, cols, nx, tile), out_shape...]
where the time goes in v5:
time: 111 us
  Pallas kernels  108 us (97%)
  local copies, waits for them, and re-layouts  1.64 us (1%)
  between operations  1.29 us (1%)
    pallas_call x1, Pallas kernels, body(): pl.pallas_call(functools.partial(kernel, rows, cols, nx, tile), out_shape...  108 us

profile of v5, /device:TPU:7, one launch (start us, length us, event | category | flops | bytes accessed | tf_op | source)
XLA Modules:
  0.0 111.3 jit_solution(1916509394417310108)
XLA Ops:
  1.3 108.3 %shard_map.59 = f32[2,40,640]{2,1,0:T(8,128)} custom-call(bf16[640,4096]{1,0:T(8,128)(2,1)} %bitcast.3, bf16[2,64,64]{2,1,0:T(8,128)(2,1)} %bitcast.4, bf16[2,64,64]{2,1,0:T(8,128)(2,1)} %bitcast.5, s32[1,1]{1,0:T(1,128)S(6)} %copy.6.live), custom_call_target="tpu_custom_call" | custom-call | tf_op jit(solution)/shard_map/pallas_call | solution.py:614
  109.6 1.6 %fusion = (f32[1,40,640]{2,1,0:T(8,128)}, f32[1,40,640]{2,1,0:T(8,128)}) fusion(f32[2,40,640]{2,1,0:T(8,128)} %shard_map.59), kind=kLoop, calls=%fused_computation | loop fusion | bytes 409600 | tf_op jit(solution)/shard_map/slice | solution.py:644

commit v6 on v5

--- a/solution.py
+++ b/solution.py
@@ -24,7 +24,7 @@
 
 
 def shares(width, ny):
-    weight = [2 if k == 1 and ny > 2 else 3 for k in range(ny)]
+    weight = [1] * ny
     edges = [width // 128 * sum(weight[:k]) // sum(weight) * 128 for k in range(ny + 1)]
     return {k: (edges[k], edges[k + 1] - edges[k]) for k in range(ny)}
 
@@ -65,7 +65,7 @@
         is_rel = is_rel | (l == half + 2 * k)
 
     lead, tail = lax.rem(n, nx) == 0, lax.rem(n, nx) == nx - 1
-    src_y, rel_y, dst_y = odd & lead & has_dn, odd & tail & (n >= nx), odd & tail & has_up
+    src_y, rel_y, dst_y = odd & lead & has_dn, even & tail & (n >= nx), odd & tail & has_up
     src_z, rel_z, dst_z = even & tail & has_up, even & lead & (n + nx < rows), even & lead & has_dn
 
     barrier = pltpu.get_barrier_semaphore()
@@ -85,8 +85,8 @@
     count += hello(has_up, n + 1, l) + hello(has_dn, n - 1, l)
     count += hello(has_dn & even, n - 1, l + 1) + hello(has_up & odd, n + 1, l - 1)
     count += hello(always, n, z_peer) + hello(is_rel, n, half - 1)
-    count += hello(src_y, n + nx - 1, l) + hello(rel_y, n - nx + 1, l)
-    count += hello(rel_y, n - nx, l) + hello(dst_y, n + nx, l)
+    count += hello(src_y, n + nx - 1, l - 1) + hello(rel_y, n - nx + 1, l + 1)
+    count += hello(rel_y, n - nx, l + 1) + hello(dst_y, n + nx, l - 1)
     count += hello(src_z, n - nx + 1, l) + hello(rel_z, n + nx - 1, l)
     count += hello(rel_z, n + nx, l) + hello(dst_z, n - nx, l)
     for k in range(1, ny):
@@ -161,10 +161,10 @@
         return remote(side_y(y_hbm, i, 0), side_y(yd, i, 0), yw_s.at[i, 0], yw_r.at[i, 0], n - 1, l)
 
     def yw_out(i):
-        return remote(side_y(y_hbm, i, 1), rely.at[i], yw_s.at[i, 1], ry_r.at[i], n + nx - 1, l)
+        return remote(side_y(y_hbm, i, 1), rely.at[i], yw_s.at[i, 1], ry_r.at[i], n + nx - 1, l - 1)
 
     def yw_on(i):
-        return remote(rely.at[i], side_y(yd, i, 1), ry_s.at[i], yw_r.at[i, 1], n - nx, l)
+        return remote(rely.at[i], side_y(yd, i, 1), ry_s.at[i], yw_r.at[i, 1], n - nx, l + 1)
 
     def zw_direct(i):
         return remote(side_z(zt, i, 0), side_z(zin, i, 0), zw_s.at[i, 0], zw_r.at[i, 0], n + 1, l)
@@ -185,11 +185,8 @@
     @pl.when(src_y)
     def _():
         for i in range(nch):
-            if i == nch - 1:
-                to_down(i).start()
-            else:
-                yw_direct(i).start()
-                yw_out(i).start()
+            yw_direct(i).start()
+            yw_out(i).start()
 
     @pl.when(plain_y)
     def _():
@@ -374,7 +371,12 @@
                     part_on(i, k).start()
         each(first)
 
-        def pass_z(i):
+        def pass_on(i):
+            @pl.when(rel_y)
+            def _():
+                yw_out(i).wait_recv()
+                yw_on(i).start()
+
             @pl.when(rel_z)
             def _():
                 zw_out(i).wait_recv()
@@ -385,8 +387,8 @@
             for at, k in ((2, 0), (4, 1)):
                 @pl.when(i == min(at, nch - 1))
                 def _():
-                    if k < nch - 1:
-                        pass_z(k)
+                    if k < nch:
+                        pass_on(k)
         each(halves)
 
         def second(i):
@@ -395,8 +397,8 @@
             for at, k in ((1, 2), (4, 3)):
                 @pl.when(i == min(at, nch - 1))
                 def _():
-                    if k < nch - 1:
-                        pass_z(k)
+                    if k < nch:
+                        pass_on(k)
         each(second)
 
         def third(i):
@@ -416,10 +418,9 @@
                 scatter_n_even(i)
 
             if nch > 4:
-                @pl.when(i == 2)
-                def _():
-                    pass_z(4)
-
+                @pl.when(i == 3)
+                def _():
+                    pass_on(4)
         each(third)
 
     @pl.when(odd)
@@ -433,13 +434,6 @@
         @pl.when(has_up)
         def _():
             remote(bdo.at[1], bdor, g_s.at[1], g_r.at[1], n, l).wait_recv()
-
-        def pass_y(i):
-            @pl.when(rel_y)
-            def _():
-                yw_out(i).wait_recv()
-                yw_on(i).start()
-        pass_y(0)
 
         def step(i):
             @pl.when(has_right)
@@ -469,18 +463,14 @@
 
             settle(i)
 
-            @pl.when(i < nch - 2)
-            def _():
-                pass_y(i + 1)
-
             @pl.when(has_up)
             def _():
-                @pl.when(tail & (i < nch - 1))
+                @pl.when(tail)
                 def _():
                     yw_direct(i).wait_recv()
                     yw_on(i).wait_recv()
 
-                @pl.when(jnp.logical_not(tail & (i < nch - 1)))
+                @pl.when(jnp.logical_not(tail))
                 def _():
                     remote(chunk(y_hbm, i), chunk(yd, i), yd_s.at[i], yd_r.at[i], n, l).wait_recv()
                 make_x(yd, i, ((lambda: bdor[...], xb),))
@@ -554,10 +544,9 @@
 
     @pl.when(src_y)
     def _():
-        for i in range(nch - 1):
+        for i in range(nch):
             yw_direct(i).wait_send()
             yw_out(i).wait_send()
-        to_down(nch - 1).wait_send()
 
     @pl.when(src_z)
     def _():
@@ -567,7 +556,7 @@
 
     @pl.when(rel_y)
     def _():
-        for i in range(nch - 1):
+        for i in range(nch):
             yw_on(i).wait_send()
 
     @pl.when(rel_z)

time: 111 us -> 110 us (level)
  Pallas kernels: 108 us -> 106 us
    pallas_call x1, Pallas kernels: 108 us -> 106 us  [body(): pl.pallas_call(functools.partial(kernel, rows, cols, nx, tile), out_shape...]
where the time goes in v6:
time: 110 us; the launch traced here: 109 us
  Pallas kernels  106 us (96%)
  local copies, waits for them, and re-layouts  1.64 us (1%)
  between operations  1.29 us (1%)
    pallas_call x1, Pallas kernels, body(): pl.pallas_call(functools.partial(kernel, rows, cols, nx, tile), out_shape...  106 us

profile of v6, /device:TPU:7, one launch (start us, length us, event | category | flops | bytes accessed | tf_op | source)
XLA Modules:
  0.0 109.4 jit_solution(12746429959234874404)
XLA Ops:
  1.3 106.5 %shard_map.59 = f32[2,40,640]{2,1,0:T(8,128)} custom-call(bf16[640,4096]{1,0:T(8,128)(2,1)} %bitcast.3, bf16[2,64,64]{2,1,0:T(8,128)(2,1)} %bitcast.4, bf16[2,64,64]{2,1,0:T(8,128)(2,1)} %bitcast.5, s32[1,1]{1,0:T(1,128)S(6)} %copy.6.live), custom_call_target="tpu_custom_call" | custom-call | tf_op jit(solution)/shard_map/pallas_call | solution.py:603
  107.7 1.6 %fusion = (f32[1,40,640]{2,1,0:T(8,128)}, f32[1,40,640]{2,1,0:T(8,128)}) fusion(f32[2,40,640]{2,1,0:T(8,128)} %shard_map.59), kind=kLoop, calls=%fused_computation | loop fusion | bytes 409600 | tf_op jit(solution)/shard_map/slice | solution.py:633

commit v7 on v6

--- a/solution.py
+++ b/solution.py
@@ -68,6 +68,15 @@
     src_y, rel_y, dst_y = odd & lead & has_dn, even & tail & (n >= nx), odd & tail & has_up
     src_z, rel_z, dst_z = even & tail & has_up, even & lead & (n + nx < rows), even & lead & has_dn
 
+    def chunk(ref, i):
+        return ref.at[pl.ds(i * C, C), :]
+
+    def local(i):
+        return pltpu.make_async_copy(chunk(y_hbm, i), chunk(y, i), loc_sem.at[i])
+
+    for i in range(nch):
+        local(i).start()
+
     barrier = pltpu.get_barrier_semaphore()
 
     def hello(cond, r, c):
@@ -103,9 +112,6 @@
             wide[k] = jnp.where(spot[0] == spot[1], g, 0.0).astype(BF)
     pl.semaphore_wait(barrier, count)
 
-    def chunk(ref, i):
-        return ref.at[pl.ds(i * C, C), :]
-
     def remote(src, dst, ss, rs, r, c):
         return pltpu.make_async_remote_copy(
             src_ref=src, dst_ref=dst, send_sem=ss, recv_sem=rs, device_id=(r, c), device_id_type=MESH)
@@ -193,11 +199,6 @@
         for i in range(nch):
             to_down(i).start()
 
-    def local(i):
-        return pltpu.make_async_copy(chunk(y_hbm, i), chunk(y, i), loc_sem.at[i])
-
-    for i in range(nch):
-        local(i).start()
     for i in range(nch):
         local(i).wait()
 

time: 110 us -> 110 us (level)
  no operation moved by 1% of the time
where the time goes in v7:
time: 110 us; the launch traced here: 109 us
  Pallas kernels  107 us (97%)
  local copies, waits for them, and re-layouts  1.64 us (1%)
  between operations  1.29 us (1%)
    pallas_call x1, Pallas kernels, body(): pl.pallas_call(functools.partial(kernel, rows, cols, nx, tile), out_shape...  107 us

profile of v7, /device:TPU:7, one launch (start us, length us, event | category | flops | bytes accessed | tf_op | source)
XLA Modules:
  0.0 109.5 jit_solution(14887601411393550155)
XLA Ops:
  1.3 106.6 %shard_map.59 = f32[2,40,640]{2,1,0:T(8,128)} custom-call(bf16[640,4096]{1,0:T(8,128)(2,1)} %bitcast.3, bf16[2,64,64]{2,1,0:T(8,128)(2,1)} %bitcast.4, bf16[2,64,64]{2,1,0:T(8,128)(2,1)} %bitcast.5, s32[1,1]{1,0:T(1,128)S(6)} %copy.6.live), custom_call_target="tpu_custom_call" | custom-call | tf_op jit(solution)/shard_map/pallas_call | solution.py:604
  107.9 1.6 %fusion = (f32[1,40,640]{2,1,0:T(8,128)}, f32[1,40,640]{2,1,0:T(8,128)}) fusion(f32[2,40,640]{2,1,0:T(8,128)} %shard_map.59), kind=kLoop, calls=%fused_computation | loop fusion | bytes 409600 | tf_op jit(solution)/shard_map/slice | solution.py:634
